TPU v7x, 512 devices: a whole 4x8x8 slice. The times are simulated.
512 devices in a mesh: gx: 32 (over x_hi, y, core), gy: 16 (over x_lo, z).
Axes of the slice: x: 4 (x_hi: 2, x_lo: 2; x = x_hi * 2 + x_lo), y: 8, z: 8, core: 2. Of those that a mesh axis runs over, the one named last changes fastest.
Arguments:
- rhs: float32 [32, 125, 2048], P('gx', None, 'gy'), may hold values from -6 to 6
- inverse: bfloat16 [32, 125, 125, 2048], P('gx', None, None, 'gy')
- weights: float32 [32, 4, 2048], P('gx', None, 'gy'), may hold values from 0.12 to 0.3
- neighbours: int32 [32, 4, 2048], P('gx', None, 'gy'), may hold values from 0 to 383, as said below
- send_lists: int32 [32, 4, 1024], P('gx', None, 'gy'), may hold values from 0 to 127
- coloring: int32 [32, 16], P('gx', 'gy'), may hold values from 0 to 3, as said below
Outputs:
- solution: float32 [32, 125, 2048], P('gx', None, 'gy')
- norms: float32 [2], replicated
Inputs may be any that keep to these rules, and one draw needn't show every extreme that they name: `coloring`: the color of subdomain (i, j) depends only on i mod 2 and j mod 2, and the four parity classes have four different colors; which class has which color varies. `neighbours`: slots below 128 are the subdomain's own faces, the rest the received intersection faces in the order of the steps; every received slot is used by some face.
All inputs are finite; a program needn't handle non-finite values.
Results may differ from a plain program's by a relative error of at most 0.0055.
Values sent between devices are 32-bit elements; how exact they have to be, the bound alone decides.
A program may use at most 64 MiB of HBM per device.

v0:
```python
import jax
import jax.numpy as jnp
from jax import lax
from jax.sharding import Mesh
from jax.sharding import PartitionSpec as P

SWEEPS = 2
GX = ("gx_0", "gx_1", "gx_2")
GY = ("gy_0", "gy_1")
GX_GY = ("gx_0", "gx_1", "gx_2", "gy_0", "gy_1")


def extended_2(cells, sides, width):
    for axis, dim in sides:
        count = lax.axis_size(axis)
        ends = count - 1
        head = lax.slice_in_dim(cells, 0, width, axis=dim)
        tail = lax.slice_in_dim(cells, cells.shape[dim] - width, cells.shape[dim], axis=dim)
        cells = jnp.concatenate(
            [
                lax.ppermute(tail, axis, [(i, (i + 1) % count) for i in range(ends)]),
                cells,
                lax.ppermute(head, axis, [((i + 1) % count, i) for i in range(ends)]),
            ],
            axis=dim,
        )
    return cells


def by_axis(array, axes):
    for axis in axes:
        array = lax.psum(array, axis)
    return array


def gather_margin(solution, sending):
    packs = [jnp.take(solution, sending[side], axis=1) for side in range(4)]
    rows_pair = jnp.stack([packs[1], packs[0]])
    rows_full = extended_2(rows_pair, ((GX, 0),), 1)
    cols_pair = jnp.stack([packs[3], packs[2]])
    cols_full = extended_2(cols_pair, ((GY, 0),), 1)
    below, above = (rows_full[0], rows_full[3])
    left, right_side = (cols_full[0], cols_full[3])
    return jnp.concatenate([solution, below, above, left, right_side], axis=1)


def body(rhs, inverse, weights, neighbours, send_lists, coloring):
    right = rhs[0]
    blocks = inverse[0]
    coupling = weights[0]
    slots = neighbours[0]
    sending = send_lists[0]
    own_color = coloring[0, 0]
    solution = jnp.zeros(right.shape, jnp.float32)
    locals_list = []

    def update(operands):
        extended, current = operands
        couple = jnp.zeros_like(current)
        for k in range(coupling.shape[0]):
            couple = couple + coupling[k][None, :] * jnp.take(extended, slots[k], axis=1)
        source = (right + couple).astype(jnp.bfloat16)
        candidate = jnp.einsum("ijf,jf->if", blocks, source, preferred_element_type=jnp.float32)
        delta = candidate - current
        return (candidate, jnp.sum(delta * delta))

    def unchanged(operands):
        return (operands[1], jnp.zeros((), jnp.float32))

    for sweep in range(SWEEPS):
        squares = jnp.zeros((), jnp.float32)
        for color in range(4):
            extended = gather_margin(solution, sending)
            solution, increment = lax.cond(
                own_color == color, update, unchanged, (extended, solution)
            )
            squares = squares + increment
        locals_list.append(squares)
    totals = by_axis(jnp.stack(locals_list), GX_GY)
    norms = jnp.sqrt(totals)
    return (solution[None], norms)


def solution(mesh):
    split = Mesh(mesh.devices.reshape(2, 8, 2, 2, 8), ("gx_0", "gx_1", "gx_2", "gy_0", "gy_1"))
    in_specs = (
        P(GX, None, GY),
        P(GX, None, None, GY),
        P(GX, None, GY),
        P(GX, None, GY),
        P(GX, None, GY),
        P(GX, GY),
    )
    out_specs = (P(GX, None, GY), P())
    return jax.shard_map(body, mesh=split, in_specs=in_specs, out_specs=out_specs, check_vma=False)
```

profile of v0, /device:TPU:12, one launch (start us, length us, event | category | flops | bytes accessed | tf_op | source)
XLA Modules:
  0.0 304.2 jit_solution(6864680266955408566)
XLA Ops:
  9.1 4.3 %collective-permute-start.2 = (f32[1,125,64]{1,2,0:T(8,128)S(1)}, f32[1,125,64]{1,2,0:T(8,128)S(1)}, u32[]{:S(2)}, u32[]{:S(2)}) collective-permute-start(f32[1,125,64]{1,2,0:T(8,128)S(1)} %select_bitcast_fusion.29), channel_id=1, source_target_pairs={{0,1},{1,2},{2,3},{3,4},{4,5},{5,6},{6,7},{7,8},{8,9},{9,10},{10,1... | collective-permute-start | bytes 96008 | tf_op jit(solution)/shard_map/ppermute | solution.py:21
  20.2 19.5 %conditional.8 = (f32[125,128]{0,1:T(8,128)}, f32[]{:T(128)}, f32[125,128]{1,0:T(8,128)}) conditional(s32[]{:T(128)} %bitcast.108, () %tuple.78, (f32[4,128]{1,0:T(4,128)}, s32[4,128]{1,0:T(4,128)}, f32[125,384]{0,1:T(8,128)S(1)}, f32[125,128]{0,1:T(8,128)S(1)}, bf16[125,125,128]{2,1,0:T(8,128)(2,1)}) %tuple.265), branch_computations={%region_0.0_spmd.clone, %region_1.5_spmd.clone} | conditional | flops 4247167 | bytes 13183772 | solution.py:74
  24.7 7.2 %copy.42 = bf16[125,125,128]{0,1,2:T(8,128)(2,1)} copy(bf16[125,125,128]{2,1,0:T(8,128)(2,1)} %get-tuple-element.193) | data formatting | bytes 8000000 | tf_op jit(solution)/shard_map
  31.9 4.0 %fusion.5 = f32[128,1,125]{2,1,0:T(1,128)} fusion(bf16[125,125,128]{0,1,2:T(8,128)(2,1)} %copy.42, bf16[125,128,1]{0,1,2:T(8,128)(2,1)S(1)} %fusion.7), kind=kOutput, calls=%fused_computation.73 | convolution fusion | flops 4000000 | bytes 4096000 | tf_op jit(solution)/shard_map/cond/branch_1_fun/ijf,jf->if/dot_general | solution.py:63
  55.0 8.9 %collective-permute-done.7 = f32[1,125,64]{1,2,0:T(8,128)S(1)} collective-permute-done((f32[1,125,64]{1,2,0:T(8,128)S(1)}, f32[1,125,64]{1,2,0:T(8,128)S(1)}, u32[]{:S(2)}, u32[]{:S(2)}) %collective-permute-start.7) | collective-permute-done | bytes 32032 | tf_op jit(solution)/shard_map/ppermute | solution.py:23
  72.9 14.8 %collective-permute-start.10 = (f32[1,125,64]{1,2,0:T(8,128)S(1)}, f32[1,125,64]{1,2,0:T(8,128)S(1)}, u32[]{:S(2)}, u32[]{:S(2)}) collective-permute-start(f32[1,125,64]{1,2,0:T(8,128)S(1)} %select_bitcast_fusion.21), channel_id=1, source_target_pairs={{0,1},{1,2},{2,3},{3,4},{4,5},{5,6},{6,7},{7,8},{8,9},{9,10},{10,1... | collective-permute-start | bytes 96008 | tf_op jit(solution)/shard_map/ppermute | solution.py:21
  89.4 4.3 %collective-permute-done.11 = f32[1,125,64]{1,2,0:T(8,128)S(1)} collective-permute-done((f32[1,125,64]{1,2,0:T(8,128)S(1)}, f32[1,125,64]{1,2,0:T(8,128)S(1)}, u32[]{:S(2)}, u32[]{:S(2)}) %collective-permute-start.11) | collective-permute-done | bytes 32032 | tf_op jit(solution)/shard_map/ppermute | solution.py:23
  104.2 13.9 %collective-permute-start.14 = (f32[1,125,64]{1,2,0:T(8,128)S(1)}, f32[1,125,64]{1,2,0:T(8,128)S(1)}, u32[]{:S(2)}, u32[]{:S(2)}) collective-permute-start(f32[1,125,64]{1,2,0:T(8,128)S(1)} %select_bitcast_fusion.17), channel_id=1, source_target_pairs={{0,1},{1,2},{2,3},{3,4},{4,5},{5,6},{6,7},{7,8},{8,9},{9,10},{10,1... | collective-permute-start | bytes 96008 | tf_op jit(solution)/shard_map/ppermute | solution.py:21
  119.7 4.3 %collective-permute-done.15 = f32[1,125,64]{1,2,0:T(8,128)S(1)} collective-permute-done((f32[1,125,64]{1,2,0:T(8,128)S(1)}, f32[1,125,64]{1,2,0:T(8,128)S(1)}, u32[]{:S(2)}, u32[]{:S(2)}) %collective-permute-start.15) | collective-permute-done | bytes 32032 | tf_op jit(solution)/shard_map/ppermute | solution.py:23
  128.9 8.6 %collective-permute-start.16 = (f32[1,125,64]{1,2,0:T(8,128)S(1)}, f32[1,125,64]{1,2,0:T(8,128)S(1)}, u32[]{:S(2)}, u32[]{:S(2)}) collective-permute-start(f32[1,125,64]{1,2,0:T(8,128)S(1)} %select_bitcast_fusion.15), channel_id=1, source_target_pairs={{0,16},{16,32},{32,48},{48,64},{64,80},{80,96},{96,112},{112,128},... | collective-permute-start | bytes 96008 | tf_op jit(solution)/shard_map/ppermute | solution.py:21
  137.6 6.8 %collective-permute-start.17 = (f32[1,125,64]{1,2,0:T(8,128)S(1)}, f32[1,125,64]{1,2,0:T(8,128)S(1)}, u32[]{:S(2)}, u32[]{:S(2)}) collective-permute-start(f32[1,125,64]{1,2,0:T(8,128)S(1)} %select_bitcast_fusion.14), channel_id=1, source_target_pairs={{16,0},{32,16},{48,32},{64,48},{80,64},{96,80},{112,96},{128,112},... | collective-permute-start | bytes 96008 | tf_op jit(solution)/shard_map/ppermute | solution.py:23
  147.3 6.1 %collective-permute-done.19 = f32[1,125,64]{1,2,0:T(8,128)S(1)} collective-permute-done((f32[1,125,64]{1,2,0:T(8,128)S(1)}, f32[1,125,64]{1,2,0:T(8,128)S(1)}, u32[]{:S(2)}, u32[]{:S(2)}) %collective-permute-start.19) | collective-permute-done | bytes 32032 | tf_op jit(solution)/shard_map/ppermute | solution.py:23
  153.4 10.8 %conditional.12 = (f32[125,128]{1,0:T(8,128)}, f32[]{:T(128)}) conditional(s32[]{:T(128)} %bitcast.108, f32[125,128]{1,0:T(8,128)} %get-tuple-element.174, (f32[4,128]{1,0:T(4,128)}, s32[4,128]{1,0:T(4,128)}, f32[125,384]{0,1:T(8,128)S(1)}, f32[125,128]{0,1:T(8,128)S(1)}, bf16[125,125,128]{2,1,0:T(8,128)(2,1)}, ...), branch_computations={%region_12.15_spmd, %region_13.0_spmd} | conditional | flops 6263167 | bytes 5311764 | solution.py:74
  158.0 4.0 %multiply_reduce_fusion.7 = f32[128,125]{0,1:T(8,128)} fusion(f32[128,125]{0,1:T(8,128)S(1)} %copy.99, bf16[125,125,128]{2,1,0:T(8,128)(2,1)} %get-tuple-element.131), kind=kLoop, calls=%fused_computation.177 | loop fusion | flops 5984000 | bytes 4128000 | tf_op jit(solution)/shard_map/cond/branch_1_fun/ijf,jf->if/dot_general | solution.py:63
  176.2 4.9 %collective-permute-done.23 = f32[1,125,64]{1,2,0:T(8,128)S(1)} collective-permute-done((f32[1,125,64]{1,2,0:T(8,128)S(1)}, f32[1,125,64]{1,2,0:T(8,128)S(1)}, u32[]{:S(2)}, u32[]{:S(2)}) %collective-permute-start.23) | collective-permute-done | bytes 32032 | tf_op jit(solution)/shard_map/ppermute | solution.py:23
  188.0 4.4 %collective-permute-start.25 = (f32[1,125,64]{1,2,0:T(8,128)S(1)}, f32[1,125,64]{1,2,0:T(8,128)S(1)}, u32[]{:S(2)}, u32[]{:S(2)}) collective-permute-start(f32[1,125,64]{1,2,0:T(8,128)S(1)} %select_bitcast_fusion.6), channel_id=1, source_target_pairs={{16,0},{32,16},{48,32},{64,48},{80,64},{96,80},{112,96},{128,112},... | collective-permute-start | bytes 96008 | tf_op jit(solution)/shard_map/ppermute | solution.py:23
  192.5 13.1 %collective-permute-start.26 = (f32[1,125,64]{1,2,0:T(8,128)S(1)}, f32[1,125,64]{1,2,0:T(8,128)S(1)}, u32[]{:S(2)}, u32[]{:S(2)}) collective-permute-start(f32[1,125,64]{1,2,0:T(8,128)S(1)} %select_bitcast_fusion.5), channel_id=1, source_target_pairs={{0,1},{1,2},{2,3},{3,4},{4,5},{5,6},{6,7},{7,8},{8,9},{9,10},{10,1... | collective-permute-start | bytes 96008 | tf_op jit(solution)/shard_map/ppermute | solution.py:21
  207.1 4.3 %collective-permute-done.27 = f32[1,125,64]{1,2,0:T(8,128)S(1)} collective-permute-done((f32[1,125,64]{1,2,0:T(8,128)S(1)}, f32[1,125,64]{1,2,0:T(8,128)S(1)}, u32[]{:S(2)}, u32[]{:S(2)}) %collective-permute-start.27) | collective-permute-done | bytes 32032 | tf_op jit(solution)/shard_map/ppermute | solution.py:23
  222.0 14.5 %collective-permute-start.30 = (f32[1,125,64]{1,2,0:T(8,128)S(1)}, f32[1,125,64]{1,2,0:T(8,128)S(1)}, u32[]{:S(2)}, u32[]{:S(2)}) collective-permute-start(f32[1,125,64]{1,2,0:T(8,128)S(1)} %select_bitcast_fusion.1), channel_id=1, source_target_pairs={{0,1},{1,2},{2,3},{3,4},{4,5},{5,6},{6,7},{7,8},{8,9},{9,10},{10,1... | collective-permute-start | bytes 96008 | tf_op jit(solution)/shard_map/ppermute | solution.py:21
  238.1 4.3 %collective-permute-done.31 = f32[1,125,64]{1,2,0:T(8,128)S(1)} collective-permute-done((f32[1,125,64]{1,2,0:T(8,128)S(1)}, f32[1,125,64]{1,2,0:T(8,128)S(1)}, u32[]{:S(2)}, u32[]{:S(2)}) %collective-permute-start.31) | collective-permute-done | bytes 32032 | tf_op jit(solution)/shard_map/ppermute | solution.py:23
  243.9 6.4 %psum.35 = f32[2]{0:T(128)S(1)} all-reduce(f32[2]{0:T(128)S(1)} %pad_maximum_fusion), channel_id=1, replica_groups=mesh['gx_0'=2,'gx_1'=8,'gx_2'=2,'gy_0'=2,'gy_1'=8] {'gx_0'}, use_global_device_ids=true, to_apply=%region_24.27 | all-reduce | flops 2 | bytes 16 | tf_op jit(solution)/shard_map/psum | solution.py:32
  250.4 23.0 %psum.36 = f32[2]{0:T(128)S(1)} all-reduce(f32[2]{0:T(128)S(1)} %psum.35), channel_id=1, replica_groups=mesh['gx_0'=2,'gx_1'=8,'gx_2'=2,'gy_0'=2,'gy_1'=8] {'gx_1'}, use_global_device_ids=true, to_apply=%region_25.28 | all-reduce | flops 2 | bytes 16 | tf_op jit(solution)/shard_map/psum | solution.py:32
  275.8 7.2 %psum.38 = f32[2]{0:T(128)S(1)} all-reduce(f32[2]{0:T(128)S(1)} %psum.37), channel_id=1, replica_groups=mesh['gx_0'=2,'gx_1'=8,'gx_2'=2,'gy_0'=2,'gy_1'=8] {'gy_0'}, use_global_device_ids=true, to_apply=%region_27.30 | all-reduce | flops 2 | bytes 16 | tf_op jit(solution)/shard_map/psum | solution.py:32
  283.0 19.1 %psum.39 = f32[2]{0:T(128)S(1)} all-reduce(f32[2]{0:T(128)S(1)} %psum.38), channel_id=1, replica_groups=mesh['gx_0'=2,'gx_1'=8,'gx_2'=2,'gy_0'=2,'gy_1'=8] {'gy_1'}, use_global_device_ids=true, to_apply=%region_28.31 | all-reduce | flops 2 | bytes 16 | tf_op jit(solution)/shard_map/psum | solution.py:32
  (203 shorter events, 119.8 us)
Async XLA Ops:
  2.2 14.8 %collective-permute-start = (f32[1,125,64]{1,2,0:T(8,128)S(1)}, f32[1,125,64]{1,2,0:T(8,128)S(1)}, u32[]{:S(2)}, u32[]{:S(2)}) collective-permute-start(f32[1,125,64]{1,2,0:T(8,128)S(1)} %select_bitcast_fusion.31), channel_id=1, source_target_pairs={{0,16},{16,32},{32,48},{48,64},{64,80},{80,96},{96,112},{112,128},... | collective-permute-start | bytes 96008 | tf_op jit(solution)/shard_map/ppermute | solution.py:21
  4.8 12.2 %collective-permute-start.1 = (f32[1,125,64]{1,2,0:T(8,128)S(1)}, f32[1,125,64]{1,2,0:T(8,128)S(1)}, u32[]{:S(2)}, u32[]{:S(2)}) collective-permute-start(f32[1,125,64]{1,2,0:T(8,128)S(1)} %select_bitcast_fusion.30), channel_id=1, source_target_pairs={{16,0},{32,16},{48,32},{64,48},{80,64},{96,80},{112,96},{128,112},... | collective-permute-start | bytes 96008 | tf_op jit(solution)/shard_map/ppermute | solution.py:23
  9.1 7.9 %collective-permute-start.2 = (f32[1,125,64]{1,2,0:T(8,128)S(1)}, f32[1,125,64]{1,2,0:T(8,128)S(1)}, u32[]{:S(2)}, u32[]{:S(2)}) collective-permute-start(f32[1,125,64]{1,2,0:T(8,128)S(1)} %select_bitcast_fusion.29), channel_id=1, source_target_pairs={{0,1},{1,2},{2,3},{3,4},{4,5},{5,6},{6,7},{7,8},{8,9},{9,10},{10,1... | collective-permute-start | bytes 96008 | tf_op jit(solution)/shard_map/ppermute | solution.py:21
  46.4 8.4 %collective-permute-start.4 = (f32[1,125,64]{1,2,0:T(8,128)S(1)}, f32[1,125,64]{1,2,0:T(8,128)S(1)}, u32[]{:S(2)}, u32[]{:S(2)}) collective-permute-start(f32[1,125,64]{1,2,0:T(8,128)S(1)} %select_bitcast_fusion.27), channel_id=1, source_target_pairs={{0,16},{16,32},{32,48},{48,64},{64,80},{80,96},{96,112},{112,128},... | collective-permute-start | bytes 96008 | tf_op jit(solution)/shard_map/ppermute | solution.py:21
  48.4 6.4 %collective-permute-start.5 = (f32[1,125,64]{1,2,0:T(8,128)S(1)}, f32[1,125,64]{1,2,0:T(8,128)S(1)}, u32[]{:S(2)}, u32[]{:S(2)}) collective-permute-start(f32[1,125,64]{1,2,0:T(8,128)S(1)} %select_bitcast_fusion.26), channel_id=1, source_target_pairs={{16,0},{32,16},{48,32},{64,48},{80,64},{96,80},{112,96},{128,112},... | collective-permute-start | bytes 96008 | tf_op jit(solution)/shard_map/ppermute | solution.py:23
  53.5 10.4 %collective-permute-start.7 = (f32[1,125,64]{1,2,0:T(8,128)S(1)}, f32[1,125,64]{1,2,0:T(8,128)S(1)}, u32[]{:S(2)}, u32[]{:S(2)}) collective-permute-start(f32[1,125,64]{1,2,0:T(8,128)S(1)} %select_bitcast_fusion.24), channel_id=1, source_target_pairs={{1,0},{2,1},{3,2},{4,3},{5,4},{6,5},{7,6},{8,7},{9,8},{10,9},{11,1... | collective-permute-start | bytes 96008 | tf_op jit(solution)/shard_map/ppermute | solution.py:23
  67.2 21.9 %collective-permute-start.8 = (f32[1,125,64]{1,2,0:T(8,128)S(1)}, f32[1,125,64]{1,2,0:T(8,128)S(1)}, u32[]{:S(2)}, u32[]{:S(2)}) collective-permute-start(f32[1,125,64]{1,2,0:T(8,128)S(1)} %select_bitcast_fusion.23), channel_id=1, source_target_pairs={{0,16},{16,32},{32,48},{48,64},{64,80},{80,96},{96,112},{112,128},... | collective-permute-start | bytes 96008 | tf_op jit(solution)/shard_map/ppermute | solution.py:21
  69.2 19.9 %collective-permute-start.9 = (f32[1,125,64]{1,2,0:T(8,128)S(1)}, f32[1,125,64]{1,2,0:T(8,128)S(1)}, u32[]{:S(2)}, u32[]{:S(2)}) collective-permute-start(f32[1,125,64]{1,2,0:T(8,128)S(1)} %select_bitcast_fusion.22), channel_id=1, source_target_pairs={{16,0},{32,16},{48,32},{64,48},{80,64},{96,80},{112,96},{128,112},... | collective-permute-start | bytes 96008 | tf_op jit(solution)/shard_map/ppermute | solution.py:23
  72.9 16.4 %collective-permute-start.10 = (f32[1,125,64]{1,2,0:T(8,128)S(1)}, f32[1,125,64]{1,2,0:T(8,128)S(1)}, u32[]{:S(2)}, u32[]{:S(2)}) collective-permute-start(f32[1,125,64]{1,2,0:T(8,128)S(1)} %select_bitcast_fusion.21), channel_id=1, source_target_pairs={{0,1},{1,2},{2,3},{3,4},{4,5},{5,6},{6,7},{7,8},{8,9},{9,10},{10,1... | collective-permute-start | bytes 96008 | tf_op jit(solution)/shard_map/ppermute | solution.py:21
  98.5 21.0 %collective-permute-start.12 = (f32[1,125,64]{1,2,0:T(8,128)S(1)}, f32[1,125,64]{1,2,0:T(8,128)S(1)}, u32[]{:S(2)}, u32[]{:S(2)}) collective-permute-start(f32[1,125,64]{1,2,0:T(8,128)S(1)} %select_bitcast_fusion.19), channel_id=1, source_target_pairs={{0,16},{16,32},{32,48},{48,64},{64,80},{80,96},{96,112},{112,128},... | collective-permute-start | bytes 96008 | tf_op jit(solution)/shard_map/ppermute | solution.py:21
  100.5 19.0 %collective-permute-start.13 = (f32[1,125,64]{1,2,0:T(8,128)S(1)}, f32[1,125,64]{1,2,0:T(8,128)S(1)}, u32[]{:S(2)}, u32[]{:S(2)}) collective-permute-start(f32[1,125,64]{1,2,0:T(8,128)S(1)} %select_bitcast_fusion.18), channel_id=1, source_target_pairs={{16,0},{32,16},{48,32},{64,48},{80,64},{96,80},{112,96},{128,112},... | collective-permute-start | bytes 96008 | tf_op jit(solution)/shard_map/ppermute | solution.py:23
  104.2 15.5 %collective-permute-start.14 = (f32[1,125,64]{1,2,0:T(8,128)S(1)}, f32[1,125,64]{1,2,0:T(8,128)S(1)}, u32[]{:S(2)}, u32[]{:S(2)}) collective-permute-start(f32[1,125,64]{1,2,0:T(8,128)S(1)} %select_bitcast_fusion.17), channel_id=1, source_target_pairs={{0,1},{1,2},{2,3},{3,4},{4,5},{5,6},{6,7},{7,8},{8,9},{9,10},{10,1... | collective-permute-start | bytes 96008 | tf_op jit(solution)/shard_map/ppermute | solution.py:21
  128.9 18.2 %collective-permute-start.16 = (f32[1,125,64]{1,2,0:T(8,128)S(1)}, f32[1,125,64]{1,2,0:T(8,128)S(1)}, u32[]{:S(2)}, u32[]{:S(2)}) collective-permute-start(f32[1,125,64]{1,2,0:T(8,128)S(1)} %select_bitcast_fusion.15), channel_id=1, source_target_pairs={{0,16},{16,32},{32,48},{48,64},{64,80},{80,96},{96,112},{112,128},... | collective-permute-start | bytes 96008 | tf_op jit(solution)/shard_map/ppermute | solution.py:21
  137.6 9.5 %collective-permute-start.17 = (f32[1,125,64]{1,2,0:T(8,128)S(1)}, f32[1,125,64]{1,2,0:T(8,128)S(1)}, u32[]{:S(2)}, u32[]{:S(2)}) collective-permute-start(f32[1,125,64]{1,2,0:T(8,128)S(1)} %select_bitcast_fusion.14), channel_id=1, source_target_pairs={{16,0},{32,16},{48,32},{64,48},{80,64},{96,80},{112,96},{128,112},... | collective-permute-start | bytes 96008 | tf_op jit(solution)/shard_map/ppermute | solution.py:23
  145.8 7.6 %collective-permute-start.19 = (f32[1,125,64]{1,2,0:T(8,128)S(1)}, f32[1,125,64]{1,2,0:T(8,128)S(1)}, u32[]{:S(2)}, u32[]{:S(2)}) collective-permute-start(f32[1,125,64]{1,2,0:T(8,128)S(1)} %select_bitcast_fusion.12), channel_id=1, source_target_pairs={{1,0},{2,1},{3,2},{4,3},{5,4},{6,5},{7,6},{8,7},{9,8},{10,9},{11,1... | collective-permute-start | bytes 96008 | tf_op jit(solution)/shard_map/ppermute | solution.py:23
  167.6 8.4 %collective-permute-start.20 = (f32[1,125,64]{1,2,0:T(8,128)S(1)}, f32[1,125,64]{1,2,0:T(8,128)S(1)}, u32[]{:S(2)}, u32[]{:S(2)}) collective-permute-start(f32[1,125,64]{1,2,0:T(8,128)S(1)} %select_bitcast_fusion.11), channel_id=1, source_target_pairs={{0,16},{16,32},{32,48},{48,64},{64,80},{80,96},{96,112},{112,128},... | collective-permute-start | bytes 96008 | tf_op jit(solution)/shard_map/ppermute | solution.py:21
  169.6 6.4 %collective-permute-start.21 = (f32[1,125,64]{1,2,0:T(8,128)S(1)}, f32[1,125,64]{1,2,0:T(8,128)S(1)}, u32[]{:S(2)}, u32[]{:S(2)}) collective-permute-start(f32[1,125,64]{1,2,0:T(8,128)S(1)} %select_bitcast_fusion.10), channel_id=1, source_target_pairs={{16,0},{32,16},{48,32},{64,48},{80,64},{96,80},{112,96},{128,112},... | collective-permute-start | bytes 96008 | tf_op jit(solution)/shard_map/ppermute | solution.py:23
  174.7 6.4 %collective-permute-start.23 = (f32[1,125,64]{1,2,0:T(8,128)S(1)}, f32[1,125,64]{1,2,0:T(8,128)S(1)}, u32[]{:S(2)}, u32[]{:S(2)}) collective-permute-start(f32[1,125,64]{1,2,0:T(8,128)S(1)} %select_bitcast_fusion.8), channel_id=1, source_target_pairs={{1,0},{2,1},{3,2},{4,3},{5,4},{6,5},{7,6},{8,7},{9,8},{10,9},{11,1... | collective-permute-start | bytes 96008 | tf_op jit(solution)/shard_map/ppermute | solution.py:23
  186.0 20.9 %collective-permute-start.24 = (f32[1,125,64]{1,2,0:T(8,128)S(1)}, f32[1,125,64]{1,2,0:T(8,128)S(1)}, u32[]{:S(2)}, u32[]{:S(2)}) collective-permute-start(f32[1,125,64]{1,2,0:T(8,128)S(1)} %select_bitcast_fusion.7), channel_id=1, source_target_pairs={{0,16},{16,32},{32,48},{48,64},{64,80},{80,96},{96,112},{112,128},... | collective-permute-start | bytes 96008 | tf_op jit(solution)/shard_map/ppermute | solution.py:21
  188.0 18.9 %collective-permute-start.25 = (f32[1,125,64]{1,2,0:T(8,128)S(1)}, f32[1,125,64]{1,2,0:T(8,128)S(1)}, u32[]{:S(2)}, u32[]{:S(2)}) collective-permute-start(f32[1,125,64]{1,2,0:T(8,128)S(1)} %select_bitcast_fusion.6), channel_id=1, source_target_pairs={{16,0},{32,16},{48,32},{64,48},{80,64},{96,80},{112,96},{128,112},... | collective-permute-start | bytes 96008 | tf_op jit(solution)/shard_map/ppermute | solution.py:23
  192.5 14.7 %collective-permute-start.26 = (f32[1,125,64]{1,2,0:T(8,128)S(1)}, f32[1,125,64]{1,2,0:T(8,128)S(1)}, u32[]{:S(2)}, u32[]{:S(2)}) collective-permute-start(f32[1,125,64]{1,2,0:T(8,128)S(1)} %select_bitcast_fusion.5), channel_id=1, source_target_pairs={{0,1},{1,2},{2,3},{3,4},{4,5},{5,6},{6,7},{7,8},{8,9},{9,10},{10,1... | collective-permute-start | bytes 96008 | tf_op jit(solution)/shard_map/ppermute | solution.py:21
  216.3 21.6 %collective-permute-start.28 = (f32[1,125,64]{1,2,0:T(8,128)S(1)}, f32[1,125,64]{1,2,0:T(8,128)S(1)}, u32[]{:S(2)}, u32[]{:S(2)}) collective-permute-start(f32[1,125,64]{1,2,0:T(8,128)S(1)} %select_bitcast_fusion.3), channel_id=1, source_target_pairs={{0,16},{16,32},{32,48},{48,64},{64,80},{80,96},{96,112},{112,128},... | collective-permute-start | bytes 96008 | tf_op jit(solution)/shard_map/ppermute | solution.py:21
  218.3 19.6 %collective-permute-start.29 = (f32[1,125,64]{1,2,0:T(8,128)S(1)}, f32[1,125,64]{1,2,0:T(8,128)S(1)}, u32[]{:S(2)}, u32[]{:S(2)}) collective-permute-start(f32[1,125,64]{1,2,0:T(8,128)S(1)} %select_bitcast_fusion.2), channel_id=1, source_target_pairs={{16,0},{32,16},{48,32},{64,48},{80,64},{96,80},{112,96},{128,112},... | collective-permute-start | bytes 96008 | tf_op jit(solution)/shard_map/ppermute | solution.py:23
  222.0 16.1 %collective-permute-start.30 = (f32[1,125,64]{1,2,0:T(8,128)S(1)}, f32[1,125,64]{1,2,0:T(8,128)S(1)}, u32[]{:S(2)}, u32[]{:S(2)}) collective-permute-start(f32[1,125,64]{1,2,0:T(8,128)S(1)} %select_bitcast_fusion.1), channel_id=1, source_target_pairs={{0,1},{1,2},{2,3},{3,4},{4,5},{5,6},{6,7},{7,8},{8,9},{9,10},{10,1... | collective-permute-start | bytes 96008 | tf_op jit(solution)/shard_map/ppermute | solution.py:21
  (8 other events, 38.0 us)
where the time goes:
time: 307 us; the launch traced here: 304 us
  starting transfers between devices  130 us (42%)
  blocking collectives  58.2 us (19%)
  local copies, waits for them, and re-layouts  55 us (18%)
  waiting for transfers between devices  41.4 us (13%)
  other arithmetic  12.5 us (4%)
  matrix products  4 us (1%)
    ppermute x16, starting transfers between devices, extended_2(): lax.ppermute(tail, axis, [(i, (i + 1) % count) for i in range(ends)])  86.4 us
    psum x5, blocking collectives, by_axis(): array = lax.psum(array, axis)  58.2 us
    ppermute x16, starting transfers between devices, extended_2(): lax.ppermute(head, axis, [((i + 1) % count, i) for i in range(ends)])  43.2 us
    ppermute x16, waiting for transfers between devices, extended_2(): lax.ppermute(head, axis, [((i + 1) % count, i) for i in range(ends)])  40.3 us
    gather x32, local copies, waits for them, and re-layouts, gather_margin(): packs = [jnp.take(solution, sending[side], axis=1) for side in range(4)]  22.4 us
    cond x6, local copies, waits for them, and re-layouts  7.42 us
    another operation x1, local copies, waits for them, and re-layouts  7.16 us
    cond x7, local copies, waits for them, and re-layouts, body(): lax.cond(own_color == color, update, unchanged, (extended, solution))  7.13 us
  transfers between devices with their start and end apart: 32, of which 15 were waited for; matrix products, arithmetic and copies ran while one was open for 2% of the time, Pallas kernels for 0%

commit v1 on v0

--- a/solution.py
+++ b/solution.py
@@ -29,7 +29,7 @@
 
 def by_axis(array, axes):
     for axis in axes:
-        array = lax.psum(array, axis)
+        array = jnp.sum(lax.all_gather(array, axis), axis=0)
     return array
 
 

time: 307 us -> 318 us (1.036)
  local copies, waits for them, and re-layouts: 55 us -> 62.9 us
  waiting for transfers between devices: 41.4 us -> 38 us
    unnamed x0 -> x5, blocking collectives: none -> 58.2 us
    psum x5 -> x0, blocking collectives: 58.2 us -> none  [by_axis(): array = lax.psum(array, axis)]
    unnamed x33 -> x47, local copies, waits for them, and re-layouts: 1.93 us -> 9.33 us
    ppermute x16, starting transfers between devices: 86.4 us -> 89.9 us  [extended_2(): lax.ppermute(tail, axis, [(i, (i + 1) % count) for i in range(ends)])]
    ppermute x16, waiting for transfers between devices: 40.3 us -> 36.9 us  [extended_2(): lax.ppermute(head, axis, [((i + 1) % count, i) for i in range(ends)])]
  transfers between devices with their start and end apart: 32 -> 32, of which waited for: 15 -> 14; matrix products, arithmetic and copies ran while one was open for 2% -> 3% of each run, Pallas kernels for 0% -> 0%
where the time goes in v1:
time: 318 us; the launch traced here: 315 us
  starting transfers between devices  133 us (42%)
  local copies, waits for them, and re-layouts  62.9 us (20%)
  blocking collectives  58.2 us (18%)
  waiting for transfers between devices  38 us (12%)
  other arithmetic  12.7 us (4%)
  between operations  5.22 us (2%)
  matrix products  4.01 us (1%)
    ppermute x16, starting transfers between devices, extended_2(): lax.ppermute(tail, axis, [(i, (i + 1) % count) for i in range(ends)])  89.9 us
    unnamed x5, blocking collectives  58.2 us
    ppermute x16, starting transfers between devices, extended_2(): lax.ppermute(head, axis, [((i + 1) % count, i) for i in range(ends)])  43.2 us
    ppermute x16, waiting for transfers between devices, extended_2(): lax.ppermute(head, axis, [((i + 1) % count, i) for i in range(ends)])  36.9 us
    gather x32, local copies, waits for them, and re-layouts, gather_margin(): packs = [jnp.take(solution, sending[side], axis=1) for side in range(4)]  22.4 us
    unnamed x47, local copies, waits for them, and re-layouts  9.33 us
    cond x6, local copies, waits for them, and re-layouts  7.45 us
    another operation x1, local copies, waits for them, and re-layouts  7.18 us
  transfers between devices with their start and end apart: 32, of which 14 were waited for; matrix products, arithmetic and copies ran while one was open for 3% of the time, Pallas kernels for 0%

profile of v1, /device:TPU:12, one launch (start us, length us, event | category | flops | bytes accessed | tf_op | source)
XLA Modules:
  0.0 315.5 jit_solution(7645043661180347116)
XLA Ops:
  9.1 4.3 %collective-permute-start.2 = (f32[1,125,64]{1,2,0:T(8,128)S(1)}, f32[1,125,64]{1,2,0:T(8,128)S(1)}, u32[]{:S(2)}, u32[]{:S(2)}) collective-permute-start(f32[1,125,64]{1,2,0:T(8,128)S(1)} %select_bitcast_fusion.29), channel_id=1, source_target_pairs={{0,1},{1,2},{2,3},{3,4},{4,5},{5,6},{6,7},{7,8},{8,9},{9,10},{10,1... | collective-permute-start | bytes 96008 | tf_op jit(solution)/shard_map/ppermute | solution.py:21
  24.1 19.4 %conditional.8 = (f32[125,128]{0,1:T(8,128)}, f32[]{:T(128)}, f32[125,128]{1,0:T(8,128)}) conditional(s32[]{:T(128)} %bitcast.108, () %tuple.78, (f32[4,128]{1,0:T(4,128)}, s32[4,128]{1,0:T(4,128)}, f32[125,384]{0,1:T(8,128)S(1)}, f32[125,128]{0,1:T(8,128)S(1)}, bf16[125,125,128]{2,1,0:T(8,128)(2,1)}) %tuple.266), branch_computations={%region_0.0_spmd.clone, %region_1.5_spmd.clone} | conditional | flops 4247167 | bytes 13183772 | solution.py:74
  28.6 7.2 %copy.75 = bf16[125,125,128]{0,1,2:T(8,128)(2,1)} copy(bf16[125,125,128]{2,1,0:T(8,128)(2,1)} %get-tuple-element.193) | data formatting | bytes 8000000 | tf_op jit(solution)/shard_map
  35.8 4.0 %fusion.5 = f32[128,1,125]{2,1,0:T(1,128)} fusion(bf16[125,125,128]{0,1,2:T(8,128)(2,1)} %copy.75, bf16[125,128,1]{0,1,2:T(8,128)(2,1)S(1)} %fusion.7), kind=kOutput, calls=%fused_computation.73 | convolution fusion | flops 4000000 | bytes 4096000 | tf_op jit(solution)/shard_map/cond/branch_1_fun/ijf,jf->if/dot_general | solution.py:63
  58.7 8.3 %collective-permute-done.7 = f32[1,125,64]{1,2,0:T(8,128)S(1)} collective-permute-done((f32[1,125,64]{1,2,0:T(8,128)S(1)}, f32[1,125,64]{1,2,0:T(8,128)S(1)}, u32[]{:S(2)}, u32[]{:S(2)}) %collective-permute-start.7) | collective-permute-done | bytes 32032 | tf_op jit(solution)/shard_map/ppermute | solution.py:23
  76.1 14.9 %collective-permute-start.10 = (f32[1,125,64]{1,2,0:T(8,128)S(1)}, f32[1,125,64]{1,2,0:T(8,128)S(1)}, u32[]{:S(2)}, u32[]{:S(2)}) collective-permute-start(f32[1,125,64]{1,2,0:T(8,128)S(1)} %select_bitcast_fusion.21), channel_id=1, source_target_pairs={{0,1},{1,2},{2,3},{3,4},{4,5},{5,6},{6,7},{7,8},{8,9},{9,10},{10,1... | collective-permute-start | bytes 96008 | tf_op jit(solution)/shard_map/ppermute | solution.py:21
  92.7 4.3 %collective-permute-done.11 = f32[1,125,64]{1,2,0:T(8,128)S(1)} collective-permute-done((f32[1,125,64]{1,2,0:T(8,128)S(1)}, f32[1,125,64]{1,2,0:T(8,128)S(1)}, u32[]{:S(2)}, u32[]{:S(2)}) %collective-permute-start.11) | collective-permute-done | bytes 32032 | tf_op jit(solution)/shard_map/ppermute | solution.py:23
  107.6 17.2 %collective-permute-start.14 = (f32[1,125,64]{1,2,0:T(8,128)S(1)}, f32[1,125,64]{1,2,0:T(8,128)S(1)}, u32[]{:S(2)}, u32[]{:S(2)}) collective-permute-start(f32[1,125,64]{1,2,0:T(8,128)S(1)} %select_bitcast_fusion.17), channel_id=1, source_target_pairs={{0,1},{1,2},{2,3},{3,4},{4,5},{5,6},{6,7},{7,8},{8,9},{9,10},{10,1... | collective-permute-start | bytes 96008 | tf_op jit(solution)/shard_map/ppermute | solution.py:21
  126.4 4.3 %collective-permute-done.15 = f32[1,125,64]{1,2,0:T(8,128)S(1)} collective-permute-done((f32[1,125,64]{1,2,0:T(8,128)S(1)}, f32[1,125,64]{1,2,0:T(8,128)S(1)}, u32[]{:S(2)}, u32[]{:S(2)}) %collective-permute-start.15) | collective-permute-done | bytes 32032 | tf_op jit(solution)/shard_map/ppermute | solution.py:23
  135.6 8.6 %collective-permute-start.16 = (f32[1,125,64]{1,2,0:T(8,128)S(1)}, f32[1,125,64]{1,2,0:T(8,128)S(1)}, u32[]{:S(2)}, u32[]{:S(2)}) collective-permute-start(f32[1,125,64]{1,2,0:T(8,128)S(1)} %select_bitcast_fusion.15), channel_id=1, source_target_pairs={{0,16},{16,32},{32,48},{48,64},{64,80},{80,96},{96,112},{112,128},... | collective-permute-start | bytes 96008 | tf_op jit(solution)/shard_map/ppermute | solution.py:21
  144.2 6.8 %collective-permute-start.17 = (f32[1,125,64]{1,2,0:T(8,128)S(1)}, f32[1,125,64]{1,2,0:T(8,128)S(1)}, u32[]{:S(2)}, u32[]{:S(2)}) collective-permute-start(f32[1,125,64]{1,2,0:T(8,128)S(1)} %select_bitcast_fusion.14), channel_id=1, source_target_pairs={{16,0},{32,16},{48,32},{64,48},{80,64},{96,80},{112,96},{128,112},... | collective-permute-start | bytes 96008 | tf_op jit(solution)/shard_map/ppermute | solution.py:23
  154.0 6.1 %collective-permute-done.19 = f32[1,125,64]{1,2,0:T(8,128)S(1)} collective-permute-done((f32[1,125,64]{1,2,0:T(8,128)S(1)}, f32[1,125,64]{1,2,0:T(8,128)S(1)}, u32[]{:S(2)}, u32[]{:S(2)}) %collective-permute-start.19) | collective-permute-done | bytes 32032 | tf_op jit(solution)/shard_map/ppermute | solution.py:23
  160.1 10.8 %conditional.12 = (f32[125,128]{1,0:T(8,128)}, f32[]{:T(128)}) conditional(s32[]{:T(128)} %bitcast.108, f32[125,128]{1,0:T(8,128)} %get-tuple-element.174, (f32[4,128]{1,0:T(4,128)}, s32[4,128]{1,0:T(4,128)}, f32[125,384]{0,1:T(8,128)S(1)}, f32[125,128]{0,1:T(8,128)S(1)}, bf16[125,125,128]{2,1,0:T(8,128)(2,1)}, ...), branch_computations={%region_12.15_spmd, %region_13.0_spmd} | conditional | flops 6263167 | bytes 5311764 | solution.py:74
  164.7 4.0 %multiply_reduce_fusion.7 = f32[128,125]{0,1:T(8,128)} fusion(f32[128,125]{0,1:T(8,128)S(1)} %copy.132, bf16[125,125,128]{2,1,0:T(8,128)(2,1)} %get-tuple-element.131), kind=kLoop, calls=%fused_computation.177 | loop fusion | flops 5984000 | bytes 4128000 | tf_op jit(solution)/shard_map/cond/branch_1_fun/ijf,jf->if/dot_general | solution.py:63
  182.9 5.3 %collective-permute-done.23 = f32[1,125,64]{1,2,0:T(8,128)S(1)} collective-permute-done((f32[1,125,64]{1,2,0:T(8,128)S(1)}, f32[1,125,64]{1,2,0:T(8,128)S(1)}, u32[]{:S(2)}, u32[]{:S(2)}) %collective-permute-start.23) | collective-permute-done | bytes 32032 | tf_op jit(solution)/shard_map/ppermute | solution.py:23
  195.1 4.4 %collective-permute-start.25 = (f32[1,125,64]{1,2,0:T(8,128)S(1)}, f32[1,125,64]{1,2,0:T(8,128)S(1)}, u32[]{:S(2)}, u32[]{:S(2)}) collective-permute-start(f32[1,125,64]{1,2,0:T(8,128)S(1)} %select_bitcast_fusion.6), channel_id=1, source_target_pairs={{16,0},{32,16},{48,32},{64,48},{80,64},{96,80},{112,96},{128,112},... | collective-permute-start | bytes 96008 | tf_op jit(solution)/shard_map/ppermute | solution.py:23
  199.6 13.1 %collective-permute-start.26 = (f32[1,125,64]{1,2,0:T(8,128)S(1)}, f32[1,125,64]{1,2,0:T(8,128)S(1)}, u32[]{:S(2)}, u32[]{:S(2)}) collective-permute-start(f32[1,125,64]{1,2,0:T(8,128)S(1)} %select_bitcast_fusion.5), channel_id=1, source_target_pairs={{0,1},{1,2},{2,3},{3,4},{4,5},{5,6},{6,7},{7,8},{8,9},{9,10},{10,1... | collective-permute-start | bytes 96008 | tf_op jit(solution)/shard_map/ppermute | solution.py:21
  214.2 4.3 %collective-permute-done.27 = f32[1,125,64]{1,2,0:T(8,128)S(1)} collective-permute-done((f32[1,125,64]{1,2,0:T(8,128)S(1)}, f32[1,125,64]{1,2,0:T(8,128)S(1)}, u32[]{:S(2)}, u32[]{:S(2)}) %collective-permute-start.27) | collective-permute-done | bytes 32032 | tf_op jit(solution)/shard_map/ppermute | solution.py:23
  229.1 14.5 %collective-permute-start.30 = (f32[1,125,64]{1,2,0:T(8,128)S(1)}, f32[1,125,64]{1,2,0:T(8,128)S(1)}, u32[]{:S(2)}, u32[]{:S(2)}) collective-permute-start(f32[1,125,64]{1,2,0:T(8,128)S(1)} %select_bitcast_fusion.1), channel_id=1, source_target_pairs={{0,1},{1,2},{2,3},{3,4},{4,5},{5,6},{6,7},{7,8},{8,9},{9,10},{10,1... | collective-permute-start | bytes 96008 | tf_op jit(solution)/shard_map/ppermute | solution.py:21
  245.2 4.3 %collective-permute-done.31 = f32[1,125,64]{1,2,0:T(8,128)S(1)} collective-permute-done((f32[1,125,64]{1,2,0:T(8,128)S(1)}, f32[1,125,64]{1,2,0:T(8,128)S(1)}, u32[]{:S(2)}, u32[]{:S(2)}) %collective-permute-start.31) | collective-permute-done | bytes 32032 | tf_op jit(solution)/shard_map/ppermute | solution.py:23
  251.8 6.4 %all-reduce = f32[4]{0:T(128)S(1)} all-reduce(f32[4]{0:T(128)S(1)} %maximum_dynamic-update-slice_fusion), channel_id=2, replica_groups=mesh['gx_0'=2,'gx_1'=8,'gx_2'=2,'gy_0'=2,'gy_1'=8] {'gx_0'}, use_global_device_ids=true, to_apply=%add | all-reduce | flops 4 | bytes 32
  258.6 23.0 %all-reduce.1 = f32[16]{0:T(128)S(1)} all-reduce(f32[16]{0:T(128)S(1)} %dynamic-update-slice.1), channel_id=3, replica_groups=mesh['gx_0'=2,'gx_1'=8,'gx_2'=2,'gy_0'=2,'gy_1'=8] {'gx_1'}, use_global_device_ids=true, to_apply=%add.1 | all-reduce | flops 16 | bytes 128
  286.6 7.2 %all-reduce.3 = f32[4]{0:T(128)S(1)} all-reduce(f32[4]{0:T(128)S(1)} %dynamic-update-slice.3), channel_id=5, replica_groups=mesh['gx_0'=2,'gx_1'=8,'gx_2'=2,'gy_0'=2,'gy_1'=8] {'gy_0'}, use_global_device_ids=true, to_apply=%add.3 | all-reduce | flops 4 | bytes 32
  294.2 19.1 %all-reduce.4 = f32[16]{0:T(128)S(1)} all-reduce(f32[16]{0:T(128)S(1)} %dynamic-update-slice.4), channel_id=6, replica_groups=mesh['gx_0'=2,'gx_1'=8,'gx_2'=2,'gy_0'=2,'gy_1'=8] {'gy_1'}, use_global_device_ids=true, to_apply=%add.4 | all-reduce | flops 16 | bytes 128
  (227 shorter events, 124.7 us)
Async XLA Ops:
  2.2 21.8 %collective-permute-start = (f32[1,125,64]{1,2,0:T(8,128)S(1)}, f32[1,125,64]{1,2,0:T(8,128)S(1)}, u32[]{:S(2)}, u32[]{:S(2)}) collective-permute-start(f32[1,125,64]{1,2,0:T(8,128)S(1)} %select_bitcast_fusion.31), channel_id=1, source_target_pairs={{0,16},{16,32},{32,48},{48,64},{64,80},{80,96},{96,112},{112,128},... | collective-permute-start | bytes 96008 | tf_op jit(solution)/shard_map/ppermute | solution.py:21
  4.8 19.2 %collective-permute-start.1 = (f32[1,125,64]{1,2,0:T(8,128)S(1)}, f32[1,125,64]{1,2,0:T(8,128)S(1)}, u32[]{:S(2)}, u32[]{:S(2)}) collective-permute-start(f32[1,125,64]{1,2,0:T(8,128)S(1)} %select_bitcast_fusion.30), channel_id=1, source_target_pairs={{16,0},{32,16},{48,32},{64,48},{80,64},{96,80},{112,96},{128,112},... | collective-permute-start | bytes 96008 | tf_op jit(solution)/shard_map/ppermute | solution.py:23
  9.1 14.9 %collective-permute-start.2 = (f32[1,125,64]{1,2,0:T(8,128)S(1)}, f32[1,125,64]{1,2,0:T(8,128)S(1)}, u32[]{:S(2)}, u32[]{:S(2)}) collective-permute-start(f32[1,125,64]{1,2,0:T(8,128)S(1)} %select_bitcast_fusion.29), channel_id=1, source_target_pairs={{0,1},{1,2},{2,3},{3,4},{4,5},{5,6},{6,7},{7,8},{8,9},{9,10},{10,1... | collective-permute-start | bytes 96008 | tf_op jit(solution)/shard_map/ppermute | solution.py:21
  14.1 10.0 %collective-permute-start.3 = (f32[1,125,64]{1,2,0:T(8,128)S(1)}, f32[1,125,64]{1,2,0:T(8,128)S(1)}, u32[]{:S(2)}, u32[]{:S(2)}) collective-permute-start(f32[1,125,64]{1,2,0:T(8,128)S(1)} %select_bitcast_fusion.28), channel_id=1, source_target_pairs={{1,0},{2,1},{3,2},{4,3},{5,4},{6,5},{7,6},{8,7},{9,8},{10,9},{11,1... | collective-permute-start | bytes 96008 | tf_op jit(solution)/shard_map/ppermute | solution.py:23
  50.1 8.4 %collective-permute-start.4 = (f32[1,125,64]{1,2,0:T(8,128)S(1)}, f32[1,125,64]{1,2,0:T(8,128)S(1)}, u32[]{:S(2)}, u32[]{:S(2)}) collective-permute-start(f32[1,125,64]{1,2,0:T(8,128)S(1)} %select_bitcast_fusion.27), channel_id=1, source_target_pairs={{0,16},{16,32},{32,48},{48,64},{64,80},{80,96},{96,112},{112,128},... | collective-permute-start | bytes 96008 | tf_op jit(solution)/shard_map/ppermute | solution.py:21
  57.2 9.8 %collective-permute-start.7 = (f32[1,125,64]{1,2,0:T(8,128)S(1)}, f32[1,125,64]{1,2,0:T(8,128)S(1)}, u32[]{:S(2)}, u32[]{:S(2)}) collective-permute-start(f32[1,125,64]{1,2,0:T(8,128)S(1)} %select_bitcast_fusion.24), channel_id=1, source_target_pairs={{1,0},{2,1},{3,2},{4,3},{5,4},{6,5},{7,6},{8,7},{9,8},{10,9},{11,1... | collective-permute-start | bytes 96008 | tf_op jit(solution)/shard_map/ppermute | solution.py:23
  70.4 22.0 %collective-permute-start.8 = (f32[1,125,64]{1,2,0:T(8,128)S(1)}, f32[1,125,64]{1,2,0:T(8,128)S(1)}, u32[]{:S(2)}, u32[]{:S(2)}) collective-permute-start(f32[1,125,64]{1,2,0:T(8,128)S(1)} %select_bitcast_fusion.23), channel_id=1, source_target_pairs={{0,16},{16,32},{32,48},{48,64},{64,80},{80,96},{96,112},{112,128},... | collective-permute-start | bytes 96008 | tf_op jit(solution)/shard_map/ppermute | solution.py:21
  72.4 20.1 %collective-permute-start.9 = (f32[1,125,64]{1,2,0:T(8,128)S(1)}, f32[1,125,64]{1,2,0:T(8,128)S(1)}, u32[]{:S(2)}, u32[]{:S(2)}) collective-permute-start(f32[1,125,64]{1,2,0:T(8,128)S(1)} %select_bitcast_fusion.22), channel_id=1, source_target_pairs={{16,0},{32,16},{48,32},{64,48},{80,64},{96,80},{112,96},{128,112},... | collective-permute-start | bytes 96008 | tf_op jit(solution)/shard_map/ppermute | solution.py:23
  76.1 16.5 %collective-permute-start.10 = (f32[1,125,64]{1,2,0:T(8,128)S(1)}, f32[1,125,64]{1,2,0:T(8,128)S(1)}, u32[]{:S(2)}, u32[]{:S(2)}) collective-permute-start(f32[1,125,64]{1,2,0:T(8,128)S(1)} %select_bitcast_fusion.21), channel_id=1, source_target_pairs={{0,1},{1,2},{2,3},{3,4},{4,5},{5,6},{6,7},{7,8},{8,9},{9,10},{10,1... | collective-permute-start | bytes 96008 | tf_op jit(solution)/shard_map/ppermute | solution.py:21
  101.8 24.3 %collective-permute-start.12 = (f32[1,125,64]{1,2,0:T(8,128)S(1)}, f32[1,125,64]{1,2,0:T(8,128)S(1)}, u32[]{:S(2)}, u32[]{:S(2)}) collective-permute-start(f32[1,125,64]{1,2,0:T(8,128)S(1)} %select_bitcast_fusion.19), channel_id=1, source_target_pairs={{0,16},{16,32},{32,48},{48,64},{64,80},{80,96},{96,112},{112,128},... | collective-permute-start | bytes 96008 | tf_op jit(solution)/shard_map/ppermute | solution.py:21
  103.8 22.4 %collective-permute-start.13 = (f32[1,125,64]{1,2,0:T(8,128)S(1)}, f32[1,125,64]{1,2,0:T(8,128)S(1)}, u32[]{:S(2)}, u32[]{:S(2)}) collective-permute-start(f32[1,125,64]{1,2,0:T(8,128)S(1)} %select_bitcast_fusion.18), channel_id=1, source_target_pairs={{16,0},{32,16},{48,32},{64,48},{80,64},{96,80},{112,96},{128,112},... | collective-permute-start | bytes 96008 | tf_op jit(solution)/shard_map/ppermute | solution.py:23
  107.6 18.8 %collective-permute-start.14 = (f32[1,125,64]{1,2,0:T(8,128)S(1)}, f32[1,125,64]{1,2,0:T(8,128)S(1)}, u32[]{:S(2)}, u32[]{:S(2)}) collective-permute-start(f32[1,125,64]{1,2,0:T(8,128)S(1)} %select_bitcast_fusion.17), channel_id=1, source_target_pairs={{0,1},{1,2},{2,3},{3,4},{4,5},{5,6},{6,7},{7,8},{8,9},{9,10},{10,1... | collective-permute-start | bytes 96008 | tf_op jit(solution)/shard_map/ppermute | solution.py:21
  135.6 18.2 %collective-permute-start.16 = (f32[1,125,64]{1,2,0:T(8,128)S(1)}, f32[1,125,64]{1,2,0:T(8,128)S(1)}, u32[]{:S(2)}, u32[]{:S(2)}) collective-permute-start(f32[1,125,64]{1,2,0:T(8,128)S(1)} %select_bitcast_fusion.15), channel_id=1, source_target_pairs={{0,16},{16,32},{32,48},{48,64},{64,80},{80,96},{96,112},{112,128},... | collective-permute-start | bytes 96008 | tf_op jit(solution)/shard_map/ppermute | solution.py:21
  144.2 9.5 %collective-permute-start.17 = (f32[1,125,64]{1,2,0:T(8,128)S(1)}, f32[1,125,64]{1,2,0:T(8,128)S(1)}, u32[]{:S(2)}, u32[]{:S(2)}) collective-permute-start(f32[1,125,64]{1,2,0:T(8,128)S(1)} %select_bitcast_fusion.14), channel_id=1, source_target_pairs={{16,0},{32,16},{48,32},{64,48},{80,64},{96,80},{112,96},{128,112},... | collective-permute-start | bytes 96008 | tf_op jit(solution)/shard_map/ppermute | solution.py:23
  152.5 7.6 %collective-permute-start.19 = (f32[1,125,64]{1,2,0:T(8,128)S(1)}, f32[1,125,64]{1,2,0:T(8,128)S(1)}, u32[]{:S(2)}, u32[]{:S(2)}) collective-permute-start(f32[1,125,64]{1,2,0:T(8,128)S(1)} %select_bitcast_fusion.12), channel_id=1, source_target_pairs={{1,0},{2,1},{3,2},{4,3},{5,4},{6,5},{7,6},{8,7},{9,8},{10,9},{11,1... | collective-permute-start | bytes 96008 | tf_op jit(solution)/shard_map/ppermute | solution.py:23
  174.3 8.4 %collective-permute-start.20 = (f32[1,125,64]{1,2,0:T(8,128)S(1)}, f32[1,125,64]{1,2,0:T(8,128)S(1)}, u32[]{:S(2)}, u32[]{:S(2)}) collective-permute-start(f32[1,125,64]{1,2,0:T(8,128)S(1)} %select_bitcast_fusion.11), channel_id=1, source_target_pairs={{0,16},{16,32},{32,48},{48,64},{64,80},{80,96},{96,112},{112,128},... | collective-permute-start | bytes 96008 | tf_op jit(solution)/shard_map/ppermute | solution.py:21
  176.3 6.4 %collective-permute-start.21 = (f32[1,125,64]{1,2,0:T(8,128)S(1)}, f32[1,125,64]{1,2,0:T(8,128)S(1)}, u32[]{:S(2)}, u32[]{:S(2)}) collective-permute-start(f32[1,125,64]{1,2,0:T(8,128)S(1)} %select_bitcast_fusion.10), channel_id=1, source_target_pairs={{16,0},{32,16},{48,32},{64,48},{80,64},{96,80},{112,96},{128,112},... | collective-permute-start | bytes 96008 | tf_op jit(solution)/shard_map/ppermute | solution.py:23
  181.4 6.8 %collective-permute-start.23 = (f32[1,125,64]{1,2,0:T(8,128)S(1)}, f32[1,125,64]{1,2,0:T(8,128)S(1)}, u32[]{:S(2)}, u32[]{:S(2)}) collective-permute-start(f32[1,125,64]{1,2,0:T(8,128)S(1)} %select_bitcast_fusion.8), channel_id=1, source_target_pairs={{1,0},{2,1},{3,2},{4,3},{5,4},{6,5},{7,6},{8,7},{9,8},{10,9},{11,1... | collective-permute-start | bytes 96008 | tf_op jit(solution)/shard_map/ppermute | solution.py:23
  193.1 20.9 %collective-permute-start.24 = (f32[1,125,64]{1,2,0:T(8,128)S(1)}, f32[1,125,64]{1,2,0:T(8,128)S(1)}, u32[]{:S(2)}, u32[]{:S(2)}) collective-permute-start(f32[1,125,64]{1,2,0:T(8,128)S(1)} %select_bitcast_fusion.7), channel_id=1, source_target_pairs={{0,16},{16,32},{32,48},{48,64},{64,80},{80,96},{96,112},{112,128},... | collective-permute-start | bytes 96008 | tf_op jit(solution)/shard_map/ppermute | solution.py:21
  195.1 18.9 %collective-permute-start.25 = (f32[1,125,64]{1,2,0:T(8,128)S(1)}, f32[1,125,64]{1,2,0:T(8,128)S(1)}, u32[]{:S(2)}, u32[]{:S(2)}) collective-permute-start(f32[1,125,64]{1,2,0:T(8,128)S(1)} %select_bitcast_fusion.6), channel_id=1, source_target_pairs={{16,0},{32,16},{48,32},{64,48},{80,64},{96,80},{112,96},{128,112},... | collective-permute-start | bytes 96008 | tf_op jit(solution)/shard_map/ppermute | solution.py:23
  199.6 14.7 %collective-permute-start.26 = (f32[1,125,64]{1,2,0:T(8,128)S(1)}, f32[1,125,64]{1,2,0:T(8,128)S(1)}, u32[]{:S(2)}, u32[]{:S(2)}) collective-permute-start(f32[1,125,64]{1,2,0:T(8,128)S(1)} %select_bitcast_fusion.5), channel_id=1, source_target_pairs={{0,1},{1,2},{2,3},{3,4},{4,5},{5,6},{6,7},{7,8},{8,9},{9,10},{10,1... | collective-permute-start | bytes 96008 | tf_op jit(solution)/shard_map/ppermute | solution.py:21
  223.4 21.6 %collective-permute-start.28 = (f32[1,125,64]{1,2,0:T(8,128)S(1)}, f32[1,125,64]{1,2,0:T(8,128)S(1)}, u32[]{:S(2)}, u32[]{:S(2)}) collective-permute-start(f32[1,125,64]{1,2,0:T(8,128)S(1)} %select_bitcast_fusion.3), channel_id=1, source_target_pairs={{0,16},{16,32},{32,48},{48,64},{64,80},{80,96},{96,112},{112,128},... | collective-permute-start | bytes 96008 | tf_op jit(solution)/shard_map/ppermute | solution.py:21
  225.4 19.6 %collective-permute-start.29 = (f32[1,125,64]{1,2,0:T(8,128)S(1)}, f32[1,125,64]{1,2,0:T(8,128)S(1)}, u32[]{:S(2)}, u32[]{:S(2)}) collective-permute-start(f32[1,125,64]{1,2,0:T(8,128)S(1)} %select_bitcast_fusion.2), channel_id=1, source_target_pairs={{16,0},{32,16},{48,32},{64,48},{80,64},{96,80},{112,96},{128,112},... | collective-permute-start | bytes 96008 | tf_op jit(solution)/shard_map/ppermute | solution.py:23
  229.1 16.1 %collective-permute-start.30 = (f32[1,125,64]{1,2,0:T(8,128)S(1)}, f32[1,125,64]{1,2,0:T(8,128)S(1)}, u32[]{:S(2)}, u32[]{:S(2)}) collective-permute-start(f32[1,125,64]{1,2,0:T(8,128)S(1)} %select_bitcast_fusion.1), channel_id=1, source_target_pairs={{0,1},{1,2},{2,3},{3,4},{4,5},{5,6},{6,7},{7,8},{8,9},{9,10},{10,1... | collective-permute-start | bytes 96008 | tf_op jit(solution)/shard_map/ppermute | solution.py:21
  (8 other events, 38.2 us)
